TPU v7x, 256 devices: a whole 4x4x8 slice. The times are simulated.
256 devices in a mesh: seq: 16 (over z, core), ch: 16 (over y, x).
Axes of the slice: x: 4, y: 4, z: 8, core: 2. Of those that a mesh axis runs over, the one named last changes fastest.
Arguments:
- query: bfloat16 [2048, 8192], P('seq', 'ch'), may hold values from -6 to 6
- key: bfloat16 [2048, 8192], P('seq', 'ch'), may hold values from -6 to 6
- value: bfloat16 [2048, 8192], P('seq', 'ch'), may hold values from -6 to 6
- short_taps: float32 [3, 3, 8192], P(None, None, 'ch'), may hold values from -3 to 3
- decay_rate: float32 [16, 8192], P(None, 'ch'), may hold values from 0.00012207031 to 0.05
- residue: float32 [16, 8192], P(None, 'ch'), may hold values from -2 to 2
- skip_gain: float32 [8192], P('ch'), may hold values from -4 to 4
- out_weight: bfloat16 [8192, 8192], P('ch', 'seq'), may hold values from -0.09375 to 0.09375
- grad_out: bfloat16 [2048, 8192], P('seq', 'ch'), may hold values from -6 to 6
Outputs:
- mixed: bfloat16 [2048, 8192], P('seq', 'ch')
- grad_query: bfloat16 [2048, 8192], P('seq', 'ch')
- grad_key: bfloat16 [2048, 8192], P('seq', 'ch')
- grad_value: bfloat16 [2048, 8192], P('seq', 'ch')
All inputs are finite; a program needn't handle non-finite values.
Results may differ from a plain program's by a relative error of at most 0.017.
Values may be sent and summed in bfloat16 or wider, within the bound.
A program may use at most 128 MiB of HBM per device.

v0:
```python
import jax
import jax.numpy as jnp
from jax import lax
from jax.sharding import PartitionSpec as P


def from_behind(block, axis, distance):
    devices = range(lax.axis_size(axis))
    route = [(i - distance, i) for i in devices if i - distance in devices]
    return lax.ppermute(block, axis, route)


def per_device(query, key, value, short_taps, decay_rate, residue, skip_gain, out_weight, grad_out):
    tok_rows, chan_width = query.shape
    tap_count = short_taps.shape[0]
    mode_count = decay_rate.shape[0]
    highest = lax.Precision.HIGHEST
    count = lax.axis_size("seq")
    place = lax.axis_index("seq")
    columns = lax.all_gather(out_weight, "seq", axis=1, tiled=True)
    grad_full = lax.all_gather(grad_out, "ch", axis=1, tiled=True)
    streams = jnp.stack([query, key, value])
    before = from_behind(streams[:, tok_rows - (tap_count - 1) :, :], "seq", 1)
    extended = jnp.concatenate([before, streams], axis=1).astype(jnp.float32)
    featured = jnp.zeros((3, tok_rows, chan_width), jnp.float32)
    for tap_index in range(tap_count):
        begin = tap_count - 1 - tap_index
        featured = (
            featured + short_taps[tap_index][:, None, :] * extended[:, begin : begin + tok_rows, :]
        )
    q_short = featured[0]
    k_short = featured[1]
    v_short = featured[2]
    gated = k_short * v_short
    mode_scale = residue * jnp.sqrt(-jnp.expm1(-2.0 * decay_rate))
    offsets = jnp.arange(tok_rows).astype(jnp.float32)
    shrink = jnp.exp(-decay_rate[None, :, :] * offsets[:, None, None])
    grow = jnp.exp(decay_rate[None, :, :] * offsets[:, None, None])
    scaled_shrink = mode_scale[None] * shrink
    scaled_grow = mode_scale[None] * grow
    one_step = jnp.exp(-decay_rate)
    block_decay = jnp.exp(-decay_rate * tok_rows)
    rows = jnp.arange(tok_rows)
    lower = (rows[:, None] >= rows[None, :]).astype(jnp.float32)
    upper = (rows[:, None] <= rows[None, :]).astype(jnp.float32)

    def prefix(tri, weights, signal):
        spread = (weights * signal[:, None, :]).reshape(tok_rows, mode_count * chan_width)
        summed = jnp.dot(tri, spread, precision=highest, preferred_element_type=jnp.float32)
        return summed.reshape(tok_rows, mode_count, chan_width)

    fwd_sums = prefix(lower, grow, gated)
    fwd_final = shrink[tok_rows - 1] * fwd_sums[tok_rows - 1]
    grad_mixer = lax.dot_general(
        grad_full, columns, (((1,), (1,)), ((), ())), preferred_element_type=jnp.float32
    )
    grad_long = grad_mixer * q_short
    bwd_sums = prefix(upper, shrink, grad_long)
    bwd_final = bwd_sums[0]
    finals = jnp.stack([fwd_final, bwd_final]).astype(jnp.bfloat16)
    gathered = lax.all_gather(finals, "seq").astype(jnp.float32)
    source = jnp.arange(count)
    fwd_gap = place - 1 - source
    bwd_gap = source - place - 1
    fwd_weight = jnp.where(
        (fwd_gap >= 0)[:, None, None],
        jnp.exp(
            -decay_rate[None]
            * (tok_rows * jnp.maximum(fwd_gap, 0)).astype(jnp.float32)[:, None, None]
        ),
        0.0,
    )
    bwd_weight = jnp.where(
        (bwd_gap >= 0)[:, None, None],
        jnp.exp(
            -decay_rate[None]
            * (tok_rows * jnp.maximum(bwd_gap, 0)).astype(jnp.float32)[:, None, None]
        ),
        0.0,
    )
    fwd_entry = jnp.sum(fwd_weight * gathered[:, 0], axis=0) * one_step
    bwd_entry = jnp.sum(bwd_weight * gathered[:, 1], axis=0) * block_decay
    long_out = (
        jnp.sum(scaled_shrink * (fwd_sums + fwd_entry[None]), axis=1) + skip_gain[None, :] * gated
    )
    mixer = (q_short * long_out).astype(jnp.bfloat16)
    partial_value = jnp.dot(mixer, columns, preferred_element_type=jnp.float32)
    mixed = lax.psum_scatter(
        partial_value.astype(jnp.bfloat16), "ch", scatter_dimension=1, tiled=True
    )
    grad_qshort = grad_mixer * long_out
    grad_gated = (
        jnp.sum(scaled_grow * (bwd_sums + bwd_entry[None]), axis=1) + skip_gain[None, :] * grad_long
    )
    grad_stack = jnp.stack([grad_qshort, grad_gated * v_short, grad_gated * k_short])
    after = from_behind(grad_stack[:, : tap_count - 1, :], "seq", -1)
    extended_back = jnp.concatenate([grad_stack, after], axis=1)
    grads = jnp.zeros((3, tok_rows, chan_width), jnp.float32)
    for tap_index in range(tap_count):
        grads = (
            grads
            + short_taps[tap_index][:, None, :]
            * extended_back[:, tap_index : tap_index + tok_rows, :]
        )
    grads = grads.astype(jnp.bfloat16)
    return (mixed, grads[0], grads[1], grads[2])


def solution(mesh):
    in_specs = (
        P("seq", "ch"),
        P("seq", "ch"),
        P("seq", "ch"),
        P(None, None, "ch"),
        P(None, "ch"),
        P(None, "ch"),
        P("ch"),
        P("ch", "seq"),
        P("seq", "ch"),
    )
    out_specs = (P("seq", "ch"), P("seq", "ch"), P("seq", "ch"), P("seq", "ch"))
    return jax.shard_map(
        per_device, mesh=mesh, in_specs=in_specs, out_specs=out_specs, check_vma=False
    )
```

profile of v0, /device:TPU:2, one launch (start us, length us, event | category | flops | bytes accessed | tf_op | source)
XLA Modules:
  0.0 272.1 jit_solution(8991568533417485764)
XLA Ops:
  7.3 0.7 all-gather.3.cloned.1.call-update
  8.0 0.7 all-gather.5.cloned.1.call-update
  8.7 0.7 pad_maximum_fusion.3
  9.5 1.7 collective-permute-start
  11.3 0.7 slice_bitcast_fusion.10
  12.0 0.8 fusion.32
  12.8 2.6 multiply_exponential_fusion
  15.6 0.2 fusion.19
  15.8 50.0 %all-gather.3.cloned.1.call-done = bf16[128,8192]{1,0:T(8,128)(2,1)} async-done(((bf16[128,512]{1,0:T(8,128)(2,1)}), bf16[128,8192]{1,0:T(8,128)(2,1)}) %all-gather.3.cloned.1.call-update) | async-done | bytes 2097168 | tf_op jit(solution)/shard_map/all_gather | solution.py:21
  65.8 57.5 %all-gather.5.cloned.1.call-done = bf16[512,8192]{1,0:T(8,128)(2,1)} async-done(((bf16[512,512]{1,0:T(8,128)(2,1)}), bf16[512,8192]{1,0:T(8,128)(2,1)}) %all-gather.5.cloned.1.call-update) | async-done | bytes 8388624 | tf_op jit(solution)/shard_map/all_gather | solution.py:20
  123.3 7.0 %fusion.26 = (f32[128,512]{1,0:T(8,128)S(1)}, f32[128,512]{1,0:T(8,128)S(1)}, f32[128,512]{1,0:T(8,128)S(1)}) fusion(f32[3,128,512]{2,1,0:T(8,128)S(1)} %fusion.19, bf16[128,8192]{1,0:T(8,128)(2,1)} %all-gather.3.cloned.1.call-done, bf16[512,8192]{1,0:T(8,128)(2,1)} %all-gather.5.cloned.1.call-done), kind=kOutput, calls=%fused_computation.49 | convolution fusion | flops 1073872896 | bytes 12058624 | tf_op jit(solution)/shard_map/dot_general | solution.py:54
  130.3 0.5 mul.273
  130.9 3.4 %copy.20 = f32[16,8,16,512]{3,1,2,0:T(8,128)S(1)} copy(f32[16,8,16,512]{3,2,1,0:T(8,128)S(1)} %bitcast.88) | data formatting | bytes 8388608
  134.3 3.0 %fusion.4 = f32[128,8192]{1,0:T(8,128)S(1)} fusion(f32[128,8192]{1,0:T(8,128)S(1)} %bitcast.86, f32[8192]{0:T(1024)S(1)} %bitcast.98, f32[128]{0:T(128)S(1)} %iota_convert_fusion), kind=kOutput, calls=%fused_computation.7 | convolution fusion | flops 1612726272 | bytes 8421888 | tf_op jit(solution)/shard_map/dot_general | solution.py:49
  137.3 1.9 copy-done
  139.4 7.5 %copy.21 = f32[16,8,16,512]{3,2,1,0:T(8,128)} copy(f32[16,8,16,512]{3,1,2,0:T(8,128)} %bitcast.84) | data formatting | bytes 8388608
  146.9 0.5 mul.261
  147.4 3.4 %copy.17 = f32[16,8,16,512]{3,1,2,0:T(8,128)S(1)} copy(f32[16,8,16,512]{3,2,1,0:T(8,128)S(1)} %bitcast.89) | data formatting | bytes 8388608
  150.9 3.0 %fusion.8 = f32[128,8192]{1,0:T(8,128)S(1)} fusion(f32[128,8192]{1,0:T(8,128)S(1)} %bitcast.87, f32[128]{0:T(128)S(1)} %iota_convert_fusion, f32[8192]{0:T(1024)S(1)} %bitcast.97), kind=kOutput, calls=%fused_computation.11 | convolution fusion | flops 1612726272 | bytes 8421888 | tf_op jit(solution)/shard_map/dot_general | solution.py:49
  153.9 1.9 copy-done.1
  156.0 5.6 %copy.18 = f32[16,8,16,512]{3,2,1,0:T(8,128)S(1)} copy(f32[16,8,16,512]{3,1,2,0:T(8,128)} %bitcast.85) | data formatting | bytes 8388608
  161.6 0.8 fusion.29
  162.4 17.1 %all_gather.12 = bf16[16,2,16,512]{3,2,1,0:T(8,128)(2,1)S(1)} all-gather(bf16[1,2,16,512]{3,2,1,0:T(8,128)(2,1)S(1)} %pad_maximum_fusion.2), channel_id=1, replica_groups=mesh['seq'=16,'ch'=16] {'seq'}, dimensions={0}, use_global_device_ids=true | all-gather | bytes 557056 | tf_op jit(solution)/shard_map/all_gather | solution.py:61
  179.7 0.3 fusion.22
  180.1 3.8 %fusion.1 = (f32[128,512]{1,0:T(8,128)S(1)}, f32[128,512]{1,0:T(8,128)S(1)}) fusion(f32[16,8,16,512]{3,2,1,0:T(8,128)S(1)} %copy-done.2, f32[16,512]{1,0:T(8,128)S(1)} %get-tuple-element.16, f32[16,512]{1,0:T(8,128)S(1)} %copy-done.3, f32[128]{0:T(128)S(1)} %iota_convert_fusion, f32[16,512]{1,0:T(8,128)S(1)} %get-tuple-element.17, ...), kind=kLoop, calls=%fused_computation.3 | loop fusion | flops 10354688 | bytes 9077248 | tf_op jit(solution)/shard_map/reduce_sum | solution.py:93
  183.9 2.6 convolution_convert_fusion
  186.5 0.2 multiply_bitcast_fusion.1
  186.8 1.3 collective-permute-start.1
  188.1 1.8 collective-permute-done.1
  190.0 0.3 fusion.17
  190.2 0.8 slice_bitcast_fusion.5
  191.0 74.6 %reduce-scatter.2.cloned.1.call-done = bf16[128,512]{1,0:T(8,128)(2,1)} async-done(((bf16[128,8192]{1,0:T(8,128)(2,1)}), bf16[128,512]{1,0:T(8,128)(2,1)}) %reduce-scatter.2.cloned.1.call-update) | async-done | bytes 131088 | tf_op jit(solution)/shard_map/reduce_scatter | solution.py:88
  (42 shorter events, 0.8 us)
Async XLA Ops:
  7.2 8.2 %copy-start.4 = (bf16[128,512]{1,0:T(8,128)(2,1)S(1)}, bf16[128,512]{1,0:T(8,128)(2,1)}, u32[]{:S(2)}) copy-start(bf16[128,512]{1,0:T(8,128)(2,1)} %param.11) | copy-start | bytes 393220
  7.2 8.2 %copy-start.5 = (bf16[128,512]{1,0:T(8,128)(2,1)S(1)}, bf16[128,512]{1,0:T(8,128)(2,1)}, u32[]{:S(2)}) copy-start(bf16[128,512]{1,0:T(8,128)(2,1)} %param.10) | copy-start | bytes 393220
  7.2 8.2 %copy-start.6 = (bf16[128,512]{1,0:T(8,128)(2,1)S(1)}, bf16[128,512]{1,0:T(8,128)(2,1)}, u32[]{:S(2)}) copy-start(bf16[128,512]{1,0:T(8,128)(2,1)} %param.9) | copy-start | bytes 393220
  7.2 8.2 %copy-start.3 = (f32[16,512]{1,0:T(8,128)S(1)}, f32[16,512]{1,0:T(8,128)}, u32[]{:S(2)}) copy-start(f32[16,512]{1,0:T(8,128)} %param.13) | copy-start | bytes 98308
  7.2 58.6 %all-gather.3.cloned.1.call-start = ((), (), s32[]{:S(2)}) async-start(), calls=%async_computation.1 | async-start | bytes 2228224 | tf_op jit(solution)/shard_map/all_gather | solution.py:21
  7.9 115.4 %all-gather.5.cloned.1.call-start = ((), (), s32[]{:S(2)}) async-start(), calls=%async_computation.2 | async-start | bytes 8912896 | tf_op jit(solution)/shard_map/all_gather | solution.py:20
  8.7 256.9 %reduce-scatter.2.cloned.1.call-start = ((), (), s32[]{:S(2)}) async-start(), calls=%async_computation.3 | async-start | bytes 2228224 | tf_op jit(solution)/shard_map/reduce_scatter | solution.py:88
  9.5 5.9 %collective-permute-start = (bf16[3,2,512]{2,1,0:T(2,128)(2,1)S(1)}, bf16[3,2,512]{2,1,0:T(2,128)(2,1)S(1)}, u32[]{:S(2)}, u32[]{:S(2)}) collective-permute-start(bf16[3,2,512]{2,1,0:T(2,128)(2,1)S(1)} %pad_maximum_fusion.3), channel_id=1, source_target_pairs={{0,16},{16,32},{32,48},{48,64},{64,80},{80,96},{96,112},{112,128},... | collective-permute-start | bytes 18440 | tf_op jit(solution)/shard_map/ppermute | solution.py:10
  137.3 1.9 copy-start
  153.9 1.9 copy-start.1
  155.9 24.0 %copy-start.8 = (f32[16,512]{1,0:T(8,128)S(1)}, f32[16,512]{1,0:T(8,128)}, u32[]{:S(2)}) copy-start(f32[16,512]{1,0:T(8,128)} %param.14) | copy-start | bytes 98308
  155.9 24.1 %copy-start.2 = (f32[16,8,16,512]{3,2,1,0:T(8,128)S(1)}, f32[16,8,16,512]{3,2,1,0:T(8,128)}, u32[]{:S(2)}) copy-start(f32[16,8,16,512]{3,2,1,0:T(8,128)} %copy.21) | copy-start | bytes 12582916
  155.9 27.9 %slice-start = ((s8[8388608]{0:T(1024)(128)(4,1)}), s8[4194304]{0:T(1024)(128)(4,1)S(1)}, s32[]{:S(2)}) async-start(s8[8388608]{0:T(1024)(128)(4,1)} %bitcast.82), calls=%async_computation.4 | async-start | bytes 8388608
  179.5 4.4 %slice-start.1 = ((s8[8388608]{0:T(1024)(128)(4,1)}), s8[4194304]{0:T(1024)(128)(4,1)S(1)}, s32[]{:S(2)}) async-start(s8[8388608]{0:T(1024)(128)(4,1)} %bitcast.82), calls=%async_computation.5 | async-start | bytes 8388608
  180.0 3.9 %copy-start.7 = (f32[512]{0:T(512)S(1)}, f32[512]{0:T(512)}, u32[]{:S(2)}) copy-start(f32[512]{0:T(512)} %param.15) | copy-start | bytes 6148
  186.8 3.1 %collective-permute-start.1 = (f32[3,2,512]{2,1,0:T(2,128)S(1)}, f32[3,2,512]{2,1,0:T(2,128)S(1)}, u32[]{:S(2)}, u32[]{:S(2)}) collective-permute-start(f32[3,2,512]{2,1,0:T(2,128)S(1)} %slice.101), channel_id=1, source_target_pairs={{16,0},{32,16},{48,32},{64,48},{80,64},{96,80},{112,96},{128,112},... | collective-permute-start | bytes 36872 | tf_op jit(solution)/shard_map/ppermute | solution.py:10
Sparse Core Ops, SparseCore 0:
  10.4 55.3 all-gather.2
  67.6 55.6 all-gather.4
  186.7 78.8 reduce-scatter.1
where the time goes:
time: 272 us
  waiting for transfers between devices  185 us (68%)
  local copies, waits for them, and re-layouts  26.7 us (10%)
  blocking collectives  17.1 us (6%)
  matrix products  15.6 us (6%)
  between operations  14.1 us (5%)
  other arithmetic  10.1 us (4%)
  starting transfers between devices  3.14 us (1%)
    reduce_scatter x1, waiting for transfers between devices, per_device(): lax.psum_scatter(partial_value.astype(jnp.bfloat16), 'ch', scatter_dimens...  74.6 us
    all_gather x1, waiting for transfers between devices, per_device(): columns = lax.all_gather(out_weight, 'seq', axis=1, tiled=True)  57.5 us
    all_gather x1, waiting for transfers between devices, per_device(): grad_full = lax.all_gather(grad_out, 'ch', axis=1, tiled=True)  50 us
    unnamed x28, local copies, waits for them, and re-layouts  24 us
    all_gather x1, blocking collectives, per_device(): gathered = lax.all_gather(finals, 'seq').astype(jnp.float32)  17.1 us
    dot_general x1, matrix products, per_device(): lax.dot_general(grad_full, columns, (((1,), (1,)), ((), ())), preferred_e...  6.97 us
    dot_general x2, matrix products, prefix(): jnp.dot(tri, spread, precision=highest, preferred_element_type=jnp.float32)  6.02 us
  transfers between devices with their start and end apart: 5, of which 4 were waited for; matrix products, arithmetic and copies ran while one was open for 2% of the time, Pallas kernels for 0%

commit v1 on v0

--- a/solution.py
+++ b/solution.py
@@ -18,7 +18,10 @@
     count = lax.axis_size("seq")
     place = lax.axis_index("seq")
     columns = lax.all_gather(out_weight, "seq", axis=1, tiled=True)
-    grad_full = lax.all_gather(grad_out, "ch", axis=1, tiled=True)
+    devices_2 = lax.axis_size("ch")
+    blocks = jnp.stack([grad_out for _ in range(devices_2)])
+    blocks = lax.all_to_all(blocks, "ch", split_axis=0, concat_axis=0)
+    grad_full = jnp.concatenate(blocks, axis=1)
     streams = jnp.stack([query, key, value])
     before = from_behind(streams[:, tok_rows - (tap_count - 1) :, :], "seq", 1)
     extended = jnp.concatenate([before, streams], axis=1).astype(jnp.float32)

time: 272 us -> 218 us (0.80)
  waiting for transfers between devices: 185 us -> 122 us
  starting transfers between devices: 3.14 us -> 10.1 us
    all_gather x1 -> x0, waiting for transfers between devices: 50 us -> none  [per_device(): grad_full = lax.all_gather(grad_out, 'ch', axis=1, tiled=True)]
    all_gather x1, waiting for transfers between devices: 57.5 us -> 23.5 us  [per_device(): columns = lax.all_gather(out_weight, 'seq', axis=1, tiled=True)]
    all_to_all x0 -> x1, waiting for transfers between devices: none -> 21.5 us  [per_device(): blocks = lax.all_to_all(blocks, 'ch', split_axis=0, concat_axis=0)]
    all_to_all x0 -> x1, starting transfers between devices: none -> 7.48 us  [per_device(): blocks = lax.all_to_all(blocks, 'ch', split_axis=0, concat_axis=0)]
    unnamed x28 -> x49, local copies, waits for them, and re-layouts: 24 us -> 25 us
  transfers between devices with their start and end apart: 5 -> 5, of which waited for: 4 -> 4; matrix products, arithmetic and copies ran while one was open for 2% -> 4% of each run, Pallas kernels for 0% -> 0%
where the time goes in v1:
time: 218 us
  waiting for transfers between devices  122 us (56%)
  local copies, waits for them, and re-layouts  28.8 us (13%)
  blocking collectives  17.1 us (8%)
  matrix products  15.6 us (7%)
  between operations  14.6 us (7%)
  starting transfers between devices  10.1 us (5%)
  other arithmetic  9.71 us (4%)
    reduce_scatter x1, waiting for transfers between devices, per_device(): lax.psum_scatter(partial_value.astype(jnp.bfloat16), 'ch', scatter_dimens...  74.5 us
    unnamed x49, local copies, waits for them, and re-layouts  25 us
    all_gather x1, waiting for transfers between devices, per_device(): columns = lax.all_gather(out_weight, 'seq', axis=1, tiled=True)  23.5 us
    all_to_all x1, waiting for transfers between devices, per_device(): blocks = lax.all_to_all(blocks, 'ch', split_axis=0, concat_axis=0)  21.5 us
    all_gather x1, blocking collectives, per_device(): gathered = lax.all_gather(finals, 'seq').astype(jnp.float32)  17.1 us
    all_to_all x1, starting transfers between devices, per_device(): blocks = lax.all_to_all(blocks, 'ch', split_axis=0, concat_axis=0)  7.48 us
    dot_general x1, matrix products, per_device(): lax.dot_general(grad_full, columns, (((1,), (1,)), ((), ())), preferred_e...  7.01 us
    dot_general x2, matrix products, prefix(): jnp.dot(tri, spread, precision=highest, preferred_element_type=jnp.float32)  6.02 us
  transfers between devices with their start and end apart: 5, of which 4 were waited for; matrix products, arithmetic and copies ran while one was open for 4% of the time, Pallas kernels for 0%

profile of v1, /device:TPU:2, one launch (start us, length us, event | category | flops | bytes accessed | tf_op | source)
XLA Modules:
  0.0 218.0 jit_solution(8251444284375878676)
XLA Ops:
  7.3 0.7 all-gather.2.cloned.1.call-update
  8.0 1.0 copy.16
  9.0 1.7 stack.56
  10.7 7.5 %all-to-all-start = ((bf16[16,128,512]{1,2,0:T(8,128)(2,1)}), bf16[16,128,512]{1,2,0:T(8,128)(2,1)S(1)}, u32[]{:S(2)}, u32[]{:S(2)}) async-start(bf16[16,128,512]{1,2,0:T(8,128)(2,1)} %stack.56), calls=%async_computation | async-start | bytes 4194304 | tf_op jit(solution)/shard_map/all_to_all | solution.py:23
  18.3 1.3 collective-permute-start
  19.6 0.5 multiply_convert_fusion.2
  20.2 2.6 %multiply_exponential_fusion = f32[128,16,512]{2,1,0:T(8,128)} fusion(f32[128]{0:T(128)S(1)} %iota_convert_fusion, f32[16,512]{1,0:T(8,128)S(1)} %get-tuple-element.18), kind=kLoop, calls=%fused_computation.15 | loop fusion | flops 1048576 | bytes 4227584 | tf_op jit(solution)/shard_map/exp | solution.py:40
  22.8 0.6 fusion.30
  23.5 0.2 fusion.19
  23.8 21.5 %all-to-all-done = bf16[16,128,512]{1,2,0:T(8,128)(2,1)S(1)} async-done(((bf16[16,128,512]{1,2,0:T(8,128)(2,1)}), bf16[16,128,512]{1,2,0:T(8,128)(2,1)S(1)}, u32[]{:S(2)}, u32[]{:S(2)}) %all-to-all-start) | async-done | bytes 2097184 | tf_op jit(solution)/shard_map/all_to_all | solution.py:23
  45.3 23.5 %all-gather.2.cloned.1.call-done = bf16[512,8192]{1,0:T(8,128)(2,1)} async-done(((bf16[512,512]{1,0:T(8,128)(2,1)}), bf16[512,8192]{1,0:T(8,128)(2,1)}) %all-gather.2.cloned.1.call-update) | async-done | bytes 8388624 | tf_op jit(solution)/shard_map/all_gather | solution.py:20
  68.8 7.0 %fusion.26 = (f32[128,512]{1,0:T(8,128)S(1)}, f32[128,512]{1,0:T(8,128)S(1)}, f32[128,512]{1,0:T(8,128)}) fusion(f32[3,128,512]{2,1,0:T(8,128)S(1)} %fusion.19, bf16[128,8192]{0,1:T(8,128)(2,1)S(1)} %bitcast.93, bf16[512,8192]{1,0:T(8,128)(2,1)} %all-gather.2.cloned.1.call-done), kind=kOutput, calls=%fused_computation.49 | convolution fusion | flops 1073872896 | bytes 12058624 | tf_op jit(solution)/shard_map/dot_general | solution.py:57
  75.8 0.5 mul.273
  76.4 3.4 %copy.23 = f32[16,8,16,512]{3,1,2,0:T(8,128)S(1)} copy(f32[16,8,16,512]{3,2,1,0:T(8,128)S(1)} %bitcast.91) | data formatting | bytes 8388608
  79.8 3.0 %fusion.4 = f32[128,8192]{1,0:T(8,128)S(1)} fusion(f32[128,8192]{1,0:T(8,128)S(1)} %bitcast.89, f32[8192]{0:T(1024)S(1)} %bitcast.102, f32[128]{0:T(128)S(1)} %copy-done.14), kind=kOutput, calls=%fused_computation.7 | convolution fusion | flops 1612726272 | bytes 8421888 | tf_op jit(solution)/shard_map/dot_general | solution.py:52
  82.8 1.9 copy-done
  84.9 7.6 %copy.24 = f32[16,8,16,512]{3,2,1,0:T(8,128)} copy(f32[16,8,16,512]{3,1,2,0:T(8,128)} %bitcast.87) | data formatting | bytes 8388608
  92.4 0.5 mul.261
  93.0 3.4 %copy.20 = f32[16,8,16,512]{3,1,2,0:T(8,128)S(1)} copy(f32[16,8,16,512]{3,2,1,0:T(8,128)S(1)} %bitcast.92) | data formatting | bytes 8388608
  96.4 3.0 %fusion.8 = f32[128,8192]{1,0:T(8,128)S(1)} fusion(f32[128,8192]{1,0:T(8,128)S(1)} %bitcast.90, f32[128]{0:T(128)S(1)} %copy-done.14, f32[8192]{0:T(1024)S(1)} %bitcast.101), kind=kOutput, calls=%fused_computation.11 | convolution fusion | flops 1612726272 | bytes 8421888 | tf_op jit(solution)/shard_map/dot_general | solution.py:52
  99.4 1.9 copy-done.1
  101.5 5.6 %copy.21 = f32[16,8,16,512]{3,2,1,0:T(8,128)S(1)} copy(f32[16,8,16,512]{3,1,2,0:T(8,128)} %bitcast.88) | data formatting | bytes 8388608
  107.2 0.8 fusion.29
  107.9 17.1 %all_gather.8 = bf16[16,2,16,512]{3,2,1,0:T(8,128)(2,1)S(1)} all-gather(bf16[1,2,16,512]{3,2,1,0:T(8,128)(2,1)S(1)} %pad_maximum_fusion.2), channel_id=1, replica_groups=mesh['seq'=16,'ch'=16] {'seq'}, dimensions={0}, use_global_device_ids=true | all-gather | bytes 557056 | tf_op jit(solution)/shard_map/all_gather | solution.py:64
  125.2 0.3 fusion.22
  125.6 3.8 %fusion.1 = (f32[128,512]{1,0:T(8,128)S(1)}, f32[128,512]{1,0:T(8,128)S(1)}) fusion(f32[16,8,16,512]{3,2,1,0:T(8,128)S(1)} %copy-done.2, f32[16,512]{1,0:T(8,128)S(1)} %get-tuple-element.16, f32[16,512]{1,0:T(8,128)S(1)} %copy-done.4, f32[128]{0:T(128)S(1)} %copy-done.14, f32[16,512]{1,0:T(8,128)S(1)} %get-tuple-element.17, ...), kind=kLoop, calls=%fused_computation.3 | loop fusion | flops 10354688 | bytes 9077248 | tf_op jit(solution)/shard_map/reduce_sum | solution.py:96
  129.5 2.6 %convolution_convert_fusion = bf16[128,8192]{1,0:T(8,128)(2,1)} fusion(bf16[512,8192]{1,0:T(8,128)(2,1)S(1)} %bitcast.86, f32[3,128,512]{2,1,0:T(8,128)S(1)} %fusion.19, f32[128,512]{1,0:T(8,128)S(1)} %get-tuple-element.7, f32[128,512]{1,0:T(8,128)S(1)} %get-tuple-element.10, f32[512]{0:T(512)S(1)} %copy-done.10), kind=kOutput, calls=%fused_computation | convolution fusion | flops 1075052544 | bytes 11274240 | tf_op jit(solution)/shard_map/dot_general | solution.py:90
  132.4 1.3 collective-permute-start.1
  133.7 1.8 collective-permute-done.1
  135.6 0.3 fusion.17
  135.8 0.8 slice_bitcast_fusion.5
  136.6 74.5 %reduce-scatter.2.cloned.1.call-done = bf16[128,512]{1,0:T(8,128)(2,1)} async-done(((bf16[128,8192]{1,0:T(8,128)(2,1)}), bf16[128,512]{1,0:T(8,128)(2,1)}) %reduce-scatter.2.cloned.1.call-update) | async-done | bytes 131088 | tf_op jit(solution)/shard_map/reduce_scatter | solution.py:91
  (63 shorter events, 1.0 us)
Async XLA Ops:
  7.2 11.1 %copy-start.5 = (bf16[128,512]{1,0:T(8,128)(2,1)S(1)}, bf16[128,512]{1,0:T(8,128)(2,1)}, u32[]{:S(2)}) copy-start(bf16[128,512]{1,0:T(8,128)(2,1)} %param.11) | copy-start | bytes 393220
  7.2 11.1 %copy-start.6 = (bf16[128,512]{1,0:T(8,128)(2,1)S(1)}, bf16[128,512]{1,0:T(8,128)(2,1)}, u32[]{:S(2)}) copy-start(bf16[128,512]{1,0:T(8,128)(2,1)} %param.10) | copy-start | bytes 393220
  7.2 11.1 %copy-start.7 = (bf16[128,512]{1,0:T(8,128)(2,1)S(1)}, bf16[128,512]{1,0:T(8,128)(2,1)}, u32[]{:S(2)}) copy-start(bf16[128,512]{1,0:T(8,128)(2,1)} %param.9) | copy-start | bytes 393220
  7.2 12.9 %copy-start.12 = (f32[3,3,512]{2,1,0:T(4,128)S(1)}, f32[3,3,512]{2,1,0:T(4,128)}, u32[]{:S(2)}) copy-start(f32[3,3,512]{2,1,0:T(4,128)} %param.12) | copy-start | bytes 55300
  7.2 12.9 %copy-start.4 = (f32[16,512]{1,0:T(8,128)S(1)}, f32[16,512]{1,0:T(8,128)}, u32[]{:S(2)}) copy-start(f32[16,512]{1,0:T(8,128)} %param.13) | copy-start | bytes 98308
  7.2 61.6 %all-gather.2.cloned.1.call-start = ((), (), s32[]{:S(2)}) async-start(), calls=%async_computation.2 | async-start | bytes 8912896 | tf_op jit(solution)/shard_map/all_gather | solution.py:20
  10.7 34.6 %all-to-all-start = ((bf16[16,128,512]{1,2,0:T(8,128)(2,1)}), bf16[16,128,512]{1,2,0:T(8,128)(2,1)S(1)}, u32[]{:S(2)}, u32[]{:S(2)}) async-start(bf16[16,128,512]{1,2,0:T(8,128)(2,1)} %stack.56), calls=%async_computation | async-start | bytes 4194304 | tf_op jit(solution)/shard_map/all_to_all | solution.py:23
  18.2 193.0 %reduce-scatter.2.cloned.1.call-start = ((), (), s32[]{:S(2)}) async-start(), calls=%async_computation.3 | async-start | bytes 2228224 | tf_op jit(solution)/shard_map/reduce_scatter | solution.py:91
  18.3 5.1 %collective-permute-start = (bf16[3,2,512]{2,1,0:T(2,128)(2,1)S(1)}, bf16[3,2,512]{2,1,0:T(2,128)(2,1)S(1)}, u32[]{:S(2)}, u32[]{:S(2)}) collective-permute-start(bf16[3,2,512]{2,1,0:T(2,128)(2,1)S(1)} %pad_maximum_fusion.3), channel_id=1, source_target_pairs={{0,16},{16,32},{32,48},{48,64},{64,80},{80,96},{96,112},{112,128},... | collective-permute-start | bytes 18440 | tf_op jit(solution)/shard_map/ppermute | solution.py:10
  19.6 3.8 %copy-start.13 = (f32[128]{0:T(128)}, f32[128]{0:T(128)S(1)}, u32[]{:S(2)}) copy-start(f32[128]{0:T(128)S(1)} %iota_convert_fusion) | copy-start | bytes 1540
  20.2 3.6 %copy-start.8 = (f32[3,512]{1,0:T(4,128)}, f32[3,512]{1,0:T(4,128)S(1)}, u32[]{:S(2)}) copy-start(f32[3,512]{1,0:T(4,128)S(1)} %get-tuple-element.22) | copy-start | bytes 18436
  76.3 3.4 %copy-start.14 = (f32[128]{0:T(128)S(1)}, f32[128]{0:T(128)}, u32[]{:S(2)}) copy-start(f32[128]{0:T(128)} %copy-done.13) | copy-start | bytes 1540
  82.8 1.9 copy-start
  99.4 1.9 copy-start.1
  101.4 23.8 %copy-start.15 = (f32[16]{0:T(128)S(1)}, f32[16]{0:T(128)}, u32[]{:S(2)}) copy-start(f32[16]{0:T(128)} %get-tuple-element.25) | copy-start | bytes 196
  101.4 23.8 %copy-start.16 = (f32[16]{0:T(128)S(1)}, f32[16]{0:T(128)}, u32[]{:S(2)}) copy-start(f32[16]{0:T(128)} %get-tuple-element.26) | copy-start | bytes 196
  101.5 23.8 %copy-start.17 = (pred[16]{0:T(512)(128)(4,1)S(1)}, pred[16]{0:T(512)(128)(4,1)}, u32[]{:S(2)}) copy-start(pred[16]{0:T(512)(128)(4,1)} %get-tuple-element.27) | copy-start | bytes 52
  101.5 23.8 %copy-start.18 = (pred[16]{0:T(512)(128)(4,1)S(1)}, pred[16]{0:T(512)(128)(4,1)}, u32[]{:S(2)}) copy-start(pred[16]{0:T(512)(128)(4,1)} %get-tuple-element.28) | copy-start | bytes 52
  101.5 24.1 %copy-start.11 = (f32[16,512]{1,0:T(8,128)S(1)}, f32[16,512]{1,0:T(8,128)}, u32[]{:S(2)}) copy-start(f32[16,512]{1,0:T(8,128)} %param.14) | copy-start | bytes 98308
  101.5 24.1 %copy-start.2 = (f32[16,8,16,512]{3,2,1,0:T(8,128)S(1)}, f32[16,8,16,512]{3,2,1,0:T(8,128)}, u32[]{:S(2)}) copy-start(f32[16,8,16,512]{3,2,1,0:T(8,128)} %copy.24) | copy-start | bytes 12582916
  101.5 27.9 %slice-start = ((s8[8388608]{0:T(1024)(128)(4,1)}), s8[4194304]{0:T(1024)(128)(4,1)S(1)}, s32[]{:S(2)}) async-start(s8[8388608]{0:T(1024)(128)(4,1)} %bitcast.85), calls=%async_computation.4 | async-start | bytes 8388608
  125.1 4.4 %slice-start.1 = ((s8[8388608]{0:T(1024)(128)(4,1)}), s8[4194304]{0:T(1024)(128)(4,1)S(1)}, s32[]{:S(2)}) async-start(s8[8388608]{0:T(1024)(128)(4,1)} %bitcast.85), calls=%async_computation.5 | async-start | bytes 8388608
  125.6 3.8 %copy-start.10 = (f32[512]{0:T(512)S(1)}, f32[512]{0:T(512)}, u32[]{:S(2)}) copy-start(f32[512]{0:T(512)} %param.15) | copy-start | bytes 6148
  129.5 2.6 %copy-start.3 = (f32[128,512]{1,0:T(8,128)S(1)}, f32[128,512]{1,0:T(8,128)}, u32[]{:S(2)}) copy-start(f32[128,512]{1,0:T(8,128)} %get-tuple-element.24) | copy-start | bytes 786436
  132.1 3.5 %copy-start.9 = (f32[3,512]{1,0:T(4,128)S(1)}, f32[3,512]{1,0:T(4,128)}, u32[]{:S(2)}) copy-start(f32[3,512]{1,0:T(4,128)} %copy-done.8) | copy-start | bytes 18436
  132.4 3.1 %collective-permute-start.1 = (f32[3,2,512]{2,1,0:T(2,128)S(1)}, f32[3,2,512]{2,1,0:T(2,128)S(1)}, u32[]{:S(2)}, u32[]{:S(2)}) collective-permute-start(f32[3,2,512]{2,1,0:T(2,128)S(1)} %slice.101), channel_id=1, source_target_pairs={{16,0},{32,16},{48,32},{64,48},{80,64},{96,80},{112,96},{128,112},... | collective-permute-start | bytes 36872 | tf_op jit(solution)/shard_map/ppermute | solution.py:10
Sparse Core Ops, SparseCore 0:
  9.9 58.8 all-gather.1
  132.3 78.8 reduce-scatter.1
